TPU v7x, 32 devices: a whole 2x2x4 slice. The times are simulated.
32 devices in a mesh: ma: 8 (over z, y), sa: 4 (over x, core).
Axes of the slice: x: 2, y: 2, z: 4, core: 2. Of those that a mesh axis runs over, the one named last changes fastest.
Arguments:
- initial_heat_matrix: float32 [128, 128, 8192], P('ma', 'sa'), may hold values from -6 to 6
- conductivity: float32 [128, 8192], P('sa'), may hold values from 0.5 to 2
- laser_x: int32 [128, 2], P('ma'), may hold values from 0 to 127
- laser_y: int32 [128, 2], P('ma'), may hold values from 0 to 127
- pixel_cell: int32 [128, 512], P('sa', 'ma'), may hold values from 0 to 127, as said below
- observed: float32 [128, 512], P('sa', 'ma'), may hold values from -6 to 6
- obs_var: float32 [128, 512], P('sa', 'ma'), may hold values from 20 to 400
Outputs:
- analysis: float32 [128, 128, 8192], P('ma', 'sa')
Inputs may be any that keep to these rules, and one draw needn't show every extreme that they name: `pixel_cell`: pixel column j views a surface cell y of its own plane; y lies within 2 of j // 4 and in the same aligned group of 16 cells as that value.
All inputs are finite; a program needn't handle non-finite values.
Results may differ from a plain program's by a relative error of at most 0.000096.
Values sent between devices are 32-bit elements; how exact they have to be, the bound alone decides.
A program may use at most 384 MiB of HBM per device.

v0:
```python
import jax
import jax.numpy as jnp
from jax import lax
from jax.sharding import PartitionSpec as P

CELLS_DEPTHWISE = 64
step_dt = 0.025
alpha_cond = 0.05
laser_power = 12.0
beam_spot_width = 18.0


def extended(block, sides, width):
    for axis, dim in sides:
        count = lax.axis_size(axis)
        forward = [(i, i + 1) for i in range(count - 1)]
        backward = [(target, source) for source, target in forward]
        low = lax.ppermute(
            lax.slice_in_dim(block, block.shape[dim] - width, None, axis=dim), axis, forward
        )
        high = lax.ppermute(lax.slice_in_dim(block, 0, width, axis=dim), axis, backward)
        block = jnp.concatenate([low, block, high], axis=dim)
    return block


def conduct(field_ext, cond_ext, first_plane, spot_x, spot_y):
    kext = cond_ext[None] * (1.0 + alpha_cond * field_ext * field_ext)
    fpad = jnp.pad(field_ext, ((0, 0), (0, 0), (1, 1), (1, 1)))
    kpad = jnp.pad(kext, ((0, 0), (0, 0), (1, 1), (1, 1)))
    centre = fpad[:, 1:-1, 1:-1, 1:-1]
    kcentre = kpad[:, 1:-1, 1:-1, 1:-1]
    shifted = [
        (slice(2, None), slice(1, -1), slice(1, -1)),
        (slice(None, -2), slice(1, -1), slice(1, -1)),
        (slice(1, -1), slice(2, None), slice(1, -1)),
        (slice(1, -1), slice(None, -2), slice(1, -1)),
        (slice(1, -1), slice(1, -1), slice(2, None)),
        (slice(1, -1), slice(1, -1), slice(None, -2)),
    ]
    flux = jnp.zeros_like(centre)
    for pick in shifted:
        neighbour = fpad[(slice(None),) + pick]
        kneigh = kpad[(slice(None),) + pick]
        flux = flux + 0.5 * (kcentre + kneigh) * (neighbour - centre)
    width = centre.shape[1]
    rows_y = centre.shape[2]
    depth = centre.shape[3]
    xglob = first_plane + jnp.arange(width, dtype=jnp.int32)
    yglob = jnp.arange(rows_y, dtype=jnp.int32)
    delta_x = (xglob[None, :] - spot_x[:, None]).astype(jnp.float32)
    delta_y = (yglob[None, :] - spot_y[:, None]).astype(jnp.float32)
    spot = laser_power * jnp.exp(
        -(delta_x[:, :, None] ** 2 + delta_y[:, None, :] ** 2) / beam_spot_width
    )
    surface_top = (jnp.arange(depth, dtype=jnp.int32) == depth - 1).astype(jnp.float32)
    heat = spot[:, :, :, None] * surface_top[None, None, None, :]
    return centre + step_dt * (flux + heat)


def transform(block, mix):
    fmean = jnp.mean(block, axis=0)
    anom = block - fmean[None]
    return fmean[None] + jnp.einsum("jxc,jk->kxc", anom, mix, precision=lax.Precision.HIGHEST)


def lower_factor(amat):
    count = amat.shape[0]
    positions = jnp.arange(count, dtype=jnp.int32)

    def column_step(index_j, factor):
        row_j = lax.dynamic_slice_in_dim(factor, index_j, 1, 0)[0]
        row_j = jnp.where(positions < index_j, row_j, 0.0)
        column = lax.dynamic_slice_in_dim(amat, index_j, 1, 1)[:, 0]
        rest = column - jnp.dot(factor, row_j, precision=lax.Precision.HIGHEST)
        pivot = jnp.sqrt(lax.dynamic_slice_in_dim(rest, index_j, 1, 0)[0])
        fresh = jnp.where(
            positions > index_j, rest / pivot, jnp.where(positions == index_j, pivot, 0.0)
        )
        return jnp.where((positions == index_j)[None, :], fresh[:, None], factor)

    return lax.fori_loop(0, count, column_step, jnp.zeros_like(amat))


def lower_inverse(factor):
    count = factor.shape[0]
    positions = jnp.arange(count, dtype=jnp.int32)

    def row_step(index_i, inverse):
        row_i = lax.dynamic_slice_in_dim(factor, index_i, 1, 0)[0]
        pivot = lax.dynamic_slice_in_dim(row_i, index_i, 1, 0)[0]
        unit = (positions == index_i).astype(jnp.float32)
        fresh = (unit - jnp.dot(row_i, inverse, precision=lax.Precision.HIGHEST)) / pivot
        return jnp.where((positions == index_i)[:, None], fresh[None, :], inverse)

    return lax.fori_loop(0, count, row_step, jnp.zeros_like(factor))


def per_device(initial_heat_matrix, conductivity, laser_x, laser_y, pixel_cell, observed, obs_var):
    members, planes, columns = initial_heat_matrix.shape
    depth = CELLS_DEPTHWISE
    rows_y = columns // depth
    first = lax.axis_index("sa") * planes
    total_planes = planes * lax.axis_size("sa")
    field = initial_heat_matrix.reshape(members, planes, rows_y, depth)
    cond_grid = conductivity.reshape(1, planes, rows_y, depth)
    stacked = jnp.concatenate([field, cond_grid], axis=0)
    wider = extended(stacked, (("sa", 1),), 2)
    cond_wide = wider[members]
    middle = conduct(wider[:members], cond_wide, first - 1, laser_x[:, 0], laser_y[:, 0])
    plane_ids = first - 1 + jnp.arange(planes + 2, dtype=jnp.int32)
    inside = ((plane_ids >= 0) & (plane_ids < total_planes)).astype(jnp.float32)
    middle = middle * inside[None, :, None, None]
    field = conduct(middle, cond_wide[1:-1], first, laser_x[:, 1], laser_y[:, 1])
    member_states = field.reshape(members, planes, columns)
    gathered = lax.all_to_all(member_states, "ma", split_axis=2, concat_axis=0, tiled=True)
    total_members = gathered.shape[0]
    group_rows = gathered.shape[2] // depth
    surface = gathered.reshape(total_members, planes, group_rows, depth)[:, :, :, depth - 1]
    group_rows = surface.shape[2]
    local_rows = pixel_cell % group_rows
    onehot = (
        local_rows[:, None, :] == jnp.arange(group_rows, dtype=jnp.int32)[None, :, None]
    ).astype(jnp.float32)
    seen = jnp.einsum("kxy,xyj->kxj", surface, onehot, precision=lax.Precision.HIGHEST)
    seen_mean = jnp.mean(seen, axis=0)
    seen_anom = seen - seen_mean[None]
    innovation = observed - seen_mean
    weight = 1.0 / obs_var
    gram_part = jnp.einsum(
        "kxj,lxj->kl", seen_anom * weight[None], seen_anom, precision=lax.Precision.HIGHEST
    )
    proj_part = jnp.einsum(
        "kxj,xj->k", seen_anom, weight * innovation, precision=lax.Precision.HIGHEST
    )
    gram, proj = lax.psum((gram_part, proj_part), ("ma", "sa"))
    count = gram.shape[0]
    eye = jnp.eye(count, dtype=jnp.float32)
    amat = eye + gram / (count - 1)
    factor = lower_factor(amat)
    inverse = lower_inverse(factor)
    wroot = inverse.T
    middle_sol = jnp.dot(inverse, proj, precision=lax.Precision.HIGHEST)
    wmean = jnp.dot(wroot, middle_sol, precision=lax.Precision.HIGHEST) / (count - 1)
    mix = wroot + wmean[:, None]
    done = transform(gathered, mix)
    return lax.all_to_all(done, "ma", split_axis=0, concat_axis=2, tiled=True)


def solution(mesh):
    placed = (
        P("ma", "sa", None),
        P("sa", None),
        P("ma", None),
        P("ma", None),
        P("sa", "ma"),
        P("sa", "ma"),
        P("sa", "ma"),
    )
    return jax.shard_map(
        per_device, mesh=mesh, in_specs=placed, out_specs=P("ma", "sa", None), check_vma=False
    )
```

profile of v0, /device:TPU:0, one launch (start us, length us, event | category | flops | bytes accessed | tf_op | source)
XLA Modules:
  0.0 2191.7 jit_solution(17658031716975416276)
XLA Ops:
  6.5 27.0 %reshape.177 = f32[16,32,128,64]{3,2,1,0:T(8,128)} reshape(f32[16,32,8192]{2,1,0:T(8,128)} %param.11) | data formatting | bytes 33554432 | tf_op jit(solution)/shard_map/reshape | solution.py:104
  33.5 23.3 %constant_dynamic-update-slice_fusion.1 = f32[17,32,128,64]{3,2,1,0:T(8,128)} fusion(f32[16,32,128,64]{3,2,1,0:T(8,128)} %reshape.177), kind=kLoop, calls=%fused_computation.160 | loop fusion | bytes 50331648
  56.8 0.8 reshape.178
  57.7 1.5 constant_dynamic-update-slice_fusion
  59.1 4.1 fusion.104
  63.2 2.8 copy.15
  66.0 3.4 collective-permute-start
  69.4 1.7 copy.16
  71.1 1.5 collective-permute-start.1
  73.0 0.9 exponential_multiply_fusion.1
  74.0 1.8 copy.17
  75.8 1.4 collective-permute-done.1
  77.2 2.9 copy.18
  80.1 26.2 %pad_maximum_fusion = f32[17,36,128,64]{3,2,1,0:T(8,128)} fusion(f32[17,2,128,64]{3,2,1,0:T(8,128)} %copy.18, f32[17,32,128,64]{3,2,1,0:T(8,128)} %constant_dynamic-update-slice_fusion, f32[17,2,128,64]{3,2,1,0:T(8,128)S(1)} %copy.17), kind=kLoop, calls=%fused_computation.30 | loop fusion | flops 10027008 | bytes 40108032 | tf_op jit(solution)/shard_map/concatenate | solution.py:22
  106.3 3.5 maximum_bitcast_fusion
  109.8 3.2 maximum_bitcast_fusion.1
  113.0 36.7 %fusion.23 = (f32[16,36,128,64]{3,2,1,0:T(8,128)}, f32[16,36,128,64]{3,2,1,0:T(8,128)}) fusion(f32[36,128,64]{2,1,0:T(8,128)} %maximum_bitcast_fusion, f32[17,36,128,64]{3,2,1,0:T(8,128)} %pad_maximum_fusion), kind=kLoop, calls=%fused_computation.32 | loop fusion | flops 18874368 | bytes 57802752 | tf_op jit(solution)/shard_map/mul | solution.py:27
  149.7 179.5 %fusion.49 = (f32[16,34,128,64]{3,2,1,0:T(8,128)}, f32[16,34,128,64]{3,2,1,0:T(8,128)}) fusion(f32[34,128,64]{2,1,0:T(8,128)} %maximum_bitcast_fusion.1, f32[34]{0:T(128)S(1)} %and_convert_fusion, f32[64]{0:T(128)S(1)} %compare_convert_fusion, f32[16,34,128]{2,1,0:T(8,128)S(1)} %exponential_multiply_fusion, f32[16,36,128,64]{3,2,1,0:T(8,128)} %get-tuple-element.281, ...), kind=kLoop, calls=%fused_computation.66 | loop fusion | flops 178257920 | bytes 295256448 | tf_op jit(solution)/shard_map/mul | solution.py:27
  329.2 165.0 %fusion.66 = f32[16,32,128,64]{3,2,1,0:T(8,128)} fusion(f32[16,34,128,64]{3,2,1,0:T(8,128)} %get-tuple-element.278, f32[16,34,128,64]{3,2,1,0:T(8,128)} %get-tuple-element.279, f32[64]{0:T(128)S(1)} %compare_convert_fusion, f32[16,32,128]{2,1,0:T(8,128)S(1)} %copy-done.4), kind=kLoop, calls=%fused_computation.95 | loop fusion | flops 138412032 | bytes 289669376 | tf_op jit(solution)/shard_map/add | solution.py:57
  494.2 45.2 %copy.30 = f32[16,32,128,64]{1,0,3,2:T(8,128)} copy(f32[16,32,128,64]{3,2,1,0:T(8,128)} %fusion.66) | data formatting | bytes 33554432 | tf_op jit(solution)/shard_map/reshape | solution.py:114
  539.4 67.4 %reshape.193 = f32[8,1,524288]{2,1,0:T(1,128)} reshape(f32[8192,16,32]{2,1,0:T(8,128)} %bitcast.86) | data formatting | bytes 33554432
  606.7 6.0 all-to-all-start
  612.8 353.2 %all-to-all-done = f32[8,1,524288]{2,1,0:T(1,128)} async-done(((f32[8,1,524288]{2,1,0:T(1,128)}), f32[8,1,524288]{2,1,0:T(1,128)}, u32[]{:S(2)}, u32[]{:S(2)}) %all-to-all-start) | async-done | bytes 16777248 | tf_op jit(solution)/shard_map/all_to_all | solution.py:115
  966.6 50.5 %reduce.1 = f32[8,524288]{1,0:T(8,128)} reduce(f32[8,1,524288]{2,1,0:T(1,128)} %all-to-all-done, f32[]{:T(128)} %broadcast.207), dimensions={1}, to_apply=%all_to_all.26.reduce_sub_computation | reduce | bytes 33554436 | tf_op jit(solution)/shard_map/all_to_all | solution.py:115
  1017.1 55.4 %reshape.194 = f32[8192,16,32]{2,1,0:T(8,128)} reshape(f32[8,524288]{1,0:T(8,128)} %reduce.1) | data formatting | bytes 33554432
  1072.5 42.5 %copy.23 = f32[8,16,32,1024]{3,2,1,0:T(8,128)} copy(f32[8,16,32,1024]{2,1,3,0:T(8,128)} %bitcast.9) | data formatting | bytes 33554432 | tf_op jit(solution)/shard_map/all_to_all | solution.py:115
  1114.9 44.4 %copy.26 = f32[8,16,32,1024]{3,1,0,2:T(8,128)} copy(f32[8,16,32,1024]{2,1,3,0:T(8,128)} %bitcast.9) | data formatting | bytes 33554432 | tf_op jit(solution)/shard_map/all_to_all | solution.py:115
  1159.3 25.8 %reshape.180 = f32[128,32,16,64]{3,2,1,0:T(8,128)} reshape(f32[8,16,32,1024]{3,2,1,0:T(8,128)} %copy.23) | data formatting | bytes 33554432 | tf_op jit(solution)/shard_map/reshape | solution.py:118
  1185.1 25.2 %slice.190 = f32[128,32,16,1]{3,2,1,0:T(8,128)} slice(f32[128,32,16,64]{3,2,1,0:T(8,128)} %reshape.180), slice={[0:128], [0:32], [0:16], [63:64]} | slice | bytes 524288 | tf_op jit(solution)/shard_map/slice | solution.py:118
  1210.3 19.1 copy.34
  1229.4 1.2 fusion.105
  1230.6 3.3 fusion.87
  1233.9 34.8 %copy.31 = f32[16,32,8,1024]{3,2,1,0:T(8,128)} copy(f32[16,32,8,1024]{1,0,3,2:T(8,128)} %bitcast.7) | data formatting | bytes 33554432 | tf_op jit(solution)/shard_map/all_to_all | solution.py:115
  1268.7 7.9 bitcast_reduce_fusion
  1276.7 12.3 bitcast_subtract_fusion
  1289.0 0.8 convolution_bitcast_fusion.3
  1289.8 48.9 %psum.15 = f32[128]{0:T(128)S(1)} all-reduce(f32[128]{0:T(128)S(1)} %convolution_bitcast_fusion.3), channel_id=1, replica_groups=mesh['ma'=8,'sa'=4] {'ma','sa'}, use_global_device_ids=true, to_apply=%region_7.8 | all-reduce | flops 128 | bytes 1024 | tf_op jit(solution)/shard_map/psum | solution.py:135
  1338.7 24.4 %all-reduce.6.cloned.1.call-done = f32[128,128]{1,0:T(8,128)} async-done(((f32[128,128]{1,0:T(8,128)}), f32[128,128]{1,0:T(8,128)}) %all-reduce.6.cloned.1.call-update) | async-done | bytes 65552 | tf_op jit(solution)/shard_map/psum | solution.py:135
  1363.1 0.9 multiply_add_fusion
  1364.0 212.1 %while.33 = (s32[]{:T(128)}, f32[128,128]{1,0:T(8,128)S(1)}, f32[128,128]{0,1:T(8,128)S(1)}, s32[]{:T(128)}, s32[]{:T(128)}) while((s32[]{:T(128)}, f32[128,128]{1,0:T(8,128)S(1)}, f32[128,128]{0,1:T(8,128)S(1)}, s32[]{:T(128)}, s32[]{:T(128)}) %tuple.94), condition=%wide.region_4.5_spmd.clone.clone, body=%wide.region_3.4_spmd.clone.clone.sunk | while | flops 246915 | bytes 332648 | solution.py:81
  1576.2 195.6 %while.32 = (s32[]{:T(128)}, f32[128,128]{1,0:T(8,128)S(1)}, f32[128,128]{1,0:T(8,128)S(1)}, s32[]{:T(128)}, s32[]{:T(128)}, /*index=5*/s32[]{:T(128)}) while((s32[]{:T(128)}, f32[128,128]{1,0:T(8,128)S(1)}, f32[128,128]{1,0:T(8,128)S(1)}, s32[]{:T(128)}, s32[]{:T(128)}, /*index=5*/s32[]{:T(128)}) %tuple.93), condition=%wide.region_6.7_spmd.clone, body=%wide.region_5.6_spmd.clone.sunk | while | flops 246404 | bytes 200048 | solution.py:95
  1578.3 0.8 fusion.119
  1584.5 0.8 fusion.119
  1589.0 0.8 fusion.119
  1772.2 21.8 convolution_add_fusion
  1794.0 15.7 copy.27
  1809.6 368.8 %all_to_all.36 = f32[128,32,1024]{2,1,0:T(8,128)S(1)} all-to-all(f32[128,32,1024]{2,1,0:T(8,128)S(1)} %copy.27), channel_id=1, replica_groups=mesh['ma'=8,'sa'=4] {'ma'}, dimensions={0} | all-to-all | bytes 33554432 | tf_op jit(solution)/shard_map/all_to_all | solution.py:146
  2178.5 6.2 copy.35
  (1319 shorter events, 307.7 us)
Async XLA Ops:
  33.5 23.3 %copy-start.3 = (f32[32,8192]{1,0:T(8,128)S(1)}, f32[32,8192]{1,0:T(8,128)}, u32[]{:S(2)}) copy-start(f32[32,8192]{1,0:T(8,128)} %param.12) | copy-start | bytes 3145732
  33.5 39.2 %copy-start.8 = (s32[16,2]{0,1:T(2,128)S(1)}, s32[16,2]{0,1:T(2,128)}, u32[]{:S(2)}) copy-start(s32[16,2]{0,1:T(2,128)} %param.13) | copy-start | bytes 388
  33.5 39.3 %copy-start.9 = (s32[16,2]{0,1:T(2,128)S(1)}, s32[16,2]{0,1:T(2,128)}, u32[]{:S(2)}) copy-start(s32[16,2]{0,1:T(2,128)} %param.14) | copy-start | bytes 388
  66.0 8.0 collective-permute-start
  71.1 6.1 collective-permute-start.1
  106.3 3.5 copy-start
  149.7 179.5 %copy-start.4 = (f32[16,32,128]{2,1,0:T(8,128)S(1)}, f32[16,32,128]{2,1,0:T(8,128)}, u32[]{:S(2)}) copy-start(f32[16,32,128]{2,1,0:T(8,128)} %exponential_multiply_fusion.1) | copy-start | bytes 786436
  606.7 6.0 copy-start.5
  606.7 359.3 %all-to-all-start = ((f32[8,1,524288]{2,1,0:T(1,128)}), f32[8,1,524288]{2,1,0:T(1,128)}, u32[]{:S(2)}, u32[]{:S(2)}) async-start(f32[8,1,524288]{2,1,0:T(1,128)} %reshape.193), calls=%async_computation | async-start | bytes 33554432 | tf_op jit(solution)/shard_map/all_to_all | solution.py:115
  612.7 750.4 %all-reduce.6.cloned.1.call-start = ((), (), s32[]{:S(2)}) async-start(), calls=%async_computation.2 | async-start | bytes 131072 | tf_op jit(solution)/shard_map/psum | solution.py:135
  1210.3 20.3 copy-start.6
  1210.3 20.3 copy-start.7
  1268.7 95.3 %copy-start.2 = (f32[128,128]{1,0:T(8,128)S(1)}, f32[128,128]{1,0:T(8,128)}, u32[]{:S(2)}) copy-start(f32[128,128]{1,0:T(8,128)} %custom-call.1) | copy-start | bytes 196612
  1268.7 307.5 %copy-start.1 = (f32[128,128]{1,0:T(8,128)S(1)}, f32[128,128]{1,0:T(8,128)}, u32[]{:S(2)}) copy-start(f32[128,128]{1,0:T(8,128)} %custom-call) | copy-start | bytes 196612
Sparse Core Ops, SparseCore 0:
  1234.1 128.9 all-reduce.5
where the time goes:
time: 2200 us; the launch traced here: 2190 us
  local copies, waits for them, and re-layouts  605 us (28%)
  other arithmetic  514 us (23%)
  blocking collectives  418 us (19%)
  waiting for transfers between devices  379 us (17%)
  matrix products  152 us (7%)
  loops' own time  99.2 us (5%)
    all_to_all x1, blocking collectives, per_device(): return lax.all_to_all(done, 'ma', split_axis=0, concat_axis=2, tiled=True)  369 us
    all_to_all x1, waiting for transfers between devices, per_device(): lax.all_to_all(member_states, 'ma', split_axis=2, concat_axis=0, tiled=True)  353 us
    mul x4, other arithmetic, conduct(): kext = cond_ext[None] * (1.0 + alpha_cond * field_ext * field_ext)  223 us
    unnamed x25, local copies, waits for them, and re-layouts  165 us
    add x1, other arithmetic, conduct(): return centre + step_dt * (flux + heat)  165 us
    all_to_all x4, local copies, waits for them, and re-layouts, per_device(): lax.all_to_all(member_states, 'ma', split_axis=2, concat_axis=0, tiled=True)  122 us
    dot_general x128, matrix products, row_step(): jnp.dot(row_i, inverse, precision=lax.Precision.HIGHEST)  102 us
    another operation x1, loops' own time, lower_factor(): return lax.fori_loop(0, count, column_step, jnp.zeros_like(amat))  94.8 us
  transfers between devices with their start and end apart: 4, of which 3 were waited for; matrix products, arithmetic and copies ran while one was open for 3% of the time, Pallas kernels for 0%

commit v1 on v0

--- a/solution.py
+++ b/solution.py
@@ -112,7 +112,12 @@
     middle = middle * inside[None, :, None, None]
     field = conduct(middle, cond_wide[1:-1], first, laser_x[:, 1], laser_y[:, 1])
     member_states = field.reshape(members, planes, columns)
-    gathered = lax.all_to_all(member_states, "ma", split_axis=2, concat_axis=0, tiled=True)
+    gathered = jnp.concatenate(
+        lax.all_to_all(
+            jnp.stack(jnp.split(member_states, lax.axis_size("ma"), axis=2)), "ma", 0, 0
+        ),
+        axis=0,
+    )
     total_members = gathered.shape[0]
     group_rows = gathered.shape[2] // depth
     surface = gathered.reshape(total_members, planes, group_rows, depth)[:, :, :, depth - 1]

time: 2200 us -> 1930 us (0.88)
  local copies, waits for them, and re-layouts: 605 us -> 384 us
  other arithmetic: 514 us -> 459 us
  waiting for transfers between devices: 379 us -> 404 us
    all_to_all x4 -> x1, local copies, waits for them, and re-layouts: 122 us -> 15.2 us  [per_device(): lax.all_to_all(jnp.stack(jnp.split(member_states, lax.axis_size('ma'), ax...]
    unnamed x25 -> x26, local copies, waits for them, and re-layouts: 165 us -> 64.7 us
    all_to_all x1 -> x0, other arithmetic: 50.5 us -> none  [per_device(): lax.all_to_all(member_states, 'ma', split_axis=2, concat_axis=0, tiled=True)]
    another operation x0 -> x2, local copies, waits for them, and re-layouts: none -> 29.1 us  [the longest x1 26 us: per_device(): gathered.reshape(total_members, planes, group_rows, depth)]
    reshape x1 -> x0, local copies, waits for them, and re-layouts: 25.8 us -> none  [per_device(): gathered.reshape(total_members, planes, group_rows, depth)]
    psum x1, waiting for transfers between devices: 24.4 us -> 49.4 us  [per_device(): gram, proj = lax.psum((gram_part, proj_part), ('ma', 'sa'))]
  transfers between devices with their start and end apart: 4 -> 4, of which waited for: 3 -> 3; matrix products, arithmetic and copies ran while one was open for 3% -> 2% of each run, Pallas kernels for 0% -> 0%
where the time goes in v1:
time: 1930 us; the launch traced here: 1920 us
  other arithmetic  459 us (24%)
  blocking collectives  418 us (22%)
  waiting for transfers between devices  404 us (21%)
  local copies, waits for them, and re-layouts  384 us (20%)
  matrix products  141 us (7%)
  loops' own time  88.3 us (5%)
    all_to_all x1, blocking collectives, per_device(): return lax.all_to_all(done, 'ma', split_axis=0, concat_axis=2, tiled=True)  369 us
    all_to_all x1, waiting for transfers between devices, per_device(): lax.all_to_all(jnp.stack(jnp.split(member_states, lax.axis_size('ma'), ax...  353 us
    mul x4, other arithmetic, conduct(): kext = cond_ext[None] * (1.0 + alpha_cond * field_ext * field_ext)  223 us
    add x1, other arithmetic, conduct(): return centre + step_dt * (flux + heat)  165 us
    dot_general x128, matrix products, row_step(): jnp.dot(row_i, inverse, precision=lax.Precision.HIGHEST)  91.4 us
    another operation x1, loops' own time, lower_factor(): return lax.fori_loop(0, count, column_step, jnp.zeros_like(amat))  83.9 us
    dynamic_slice x128, local copies, waits for them, and re-layouts, column_step(): pivot = jnp.sqrt(lax.dynamic_slice_in_dim(rest, index_j, 1, 0)[0])  81.8 us
    dynamic_slice x128, local copies, waits for them, and re-layouts, row_step(): pivot = lax.dynamic_slice_in_dim(row_i, index_i, 1, 0)[0]  75.7 us
  transfers between devices with their start and end apart: 4, of which 3 were waited for; matrix products, arithmetic and copies ran while one was open for 2% of the time, Pallas kernels for 0%

profile of v1, /device:TPU:0, one launch (start us, length us, event | category | flops | bytes accessed | tf_op | source)
XLA Modules:
  0.0 1918.1 jit_solution(215052254243528551)
XLA Ops:
  6.5 27.0 %reshape.176 = f32[16,32,128,64]{3,2,1,0:T(8,128)} reshape(f32[16,32,8192]{2,1,0:T(8,128)} %param.11) | data formatting | bytes 33554432 | tf_op jit(solution)/shard_map/reshape | solution.py:104
  33.6 23.3 %constant_dynamic-update-slice_fusion.1 = f32[17,32,128,64]{3,2,1,0:T(8,128)} fusion(f32[16,32,128,64]{3,2,1,0:T(8,128)} %reshape.176), kind=kLoop, calls=%fused_computation.167 | loop fusion | bytes 50331648
  56.9 0.8 reshape.177
  57.7 1.5 constant_dynamic-update-slice_fusion
  59.2 4.1 fusion.112
  63.2 2.8 copy.22
  66.0 3.4 collective-permute-start
  69.4 1.7 copy.23
  71.1 1.8 collective-permute-start.1
  73.2 0.8 exponential_multiply_fusion.1
  74.2 1.8 copy.24
  76.1 1.1 collective-permute-done.1
  77.2 2.8 copy.25
  80.0 26.2 %pad_maximum_fusion = f32[17,36,128,64]{3,2,1,0:T(8,128)} fusion(f32[17,2,128,64]{3,2,1,0:T(8,128)} %copy.25, f32[17,32,128,64]{3,2,1,0:T(8,128)} %constant_dynamic-update-slice_fusion, f32[17,2,128,64]{3,2,1,0:T(8,128)S(1)} %copy.24), kind=kLoop, calls=%fused_computation.30 | loop fusion | flops 10027008 | bytes 40108032 | tf_op jit(solution)/shard_map/concatenate | solution.py:22
  106.2 3.5 maximum_bitcast_fusion
  109.6 3.2 maximum_bitcast_fusion.1
  112.9 36.7 %fusion.23 = (f32[16,36,128,64]{3,2,1,0:T(8,128)}, f32[16,36,128,64]{3,2,1,0:T(8,128)}) fusion(f32[36,128,64]{2,1,0:T(8,128)} %maximum_bitcast_fusion, f32[17,36,128,64]{3,2,1,0:T(8,128)} %pad_maximum_fusion), kind=kLoop, calls=%fused_computation.32 | loop fusion | flops 18874368 | bytes 57802752 | tf_op jit(solution)/shard_map/mul | solution.py:27
  149.6 179.5 %fusion.49 = (f32[16,34,128,64]{3,2,1,0:T(8,128)}, f32[16,34,128,64]{3,2,1,0:T(8,128)}) fusion(f32[34,128,64]{2,1,0:T(8,128)} %maximum_bitcast_fusion.1, f32[34]{0:T(128)S(1)} %and_convert_fusion, f32[64]{0:T(128)S(1)} %compare_convert_fusion, f32[16,34,128]{2,1,0:T(8,128)S(1)} %exponential_multiply_fusion, f32[16,36,128,64]{3,2,1,0:T(8,128)} %get-tuple-element.281, ...), kind=kLoop, calls=%fused_computation.66 | loop fusion | flops 178257920 | bytes 295256448 | tf_op jit(solution)/shard_map/mul | solution.py:27
  329.0 165.1 %fusion.66 = f32[16,32,128,64]{3,2,1,0:T(8,128)} fusion(f32[16,34,128,64]{3,2,1,0:T(8,128)} %get-tuple-element.278, f32[16,34,128,64]{3,2,1,0:T(8,128)} %get-tuple-element.279, f32[64]{0:T(128)S(1)} %compare_convert_fusion, f32[16,32,128]{2,1,0:T(8,128)S(1)} %copy-done.2), kind=kLoop, calls=%fused_computation.95 | loop fusion | flops 138412032 | bytes 289669376 | tf_op jit(solution)/shard_map/add | solution.py:57
  494.2 27.9 %reshape.178 = f32[16,32,8192]{2,1,0:T(8,128)} reshape(f32[16,32,128,64]{3,2,1,0:T(8,128)} %fusion.66) | data formatting | bytes 33554432 | tf_op jit(solution)/shard_map/reshape | solution.py:114
  522.1 3.2 fusion.92
  525.3 3.1 fusion.91
  528.4 3.2 fusion.90
  531.6 3.2 fusion.89
  534.8 3.2 fusion.88
  538.0 3.2 fusion.87
  541.1 3.2 fusion.86
  544.3 3.1 fusion.85
  547.4 5.8 all-to-all-start
  553.4 353.2 %all-to-all-done = f32[8,16,32,1024]{3,2,1,0:T(8,128)} async-done(((f32[8,16,32,1024]{3,2,1,0:T(8,128)}), f32[8,16,32,1024]{3,2,1,0:T(8,128)}, u32[]{:S(2)}, u32[]{:S(2)}) %all-to-all-start) | async-done | bytes 16777248 | tf_op jit(solution)/shard_map/all_to_all | solution.py:116
  906.6 26.0 %reshape_reshape.3 = f32[128,32,16,64]{3,2,1,0:T(8,128)} reshape(f32[8,16,32,1024]{3,2,1,0:T(8,128)} %all-to-all-done) | data formatting | bytes 33554432 | tf_op jit(solution)/shard_map/reshape;reshape | solution.py:123
  932.6 25.2 %slice.190 = f32[128,32,16,1]{3,2,1,0:T(8,128)} slice(f32[128,32,16,64]{3,2,1,0:T(8,128)} %reshape_reshape.3), slice={[0:128], [0:32], [0:16], [63:64]} | slice | bytes 524288 | tf_op jit(solution)/shard_map/slice | solution.py:123
  957.7 19.1 copy.34
  976.8 1.2 fusion.113
  978.0 3.3 fusion.95
  981.4 6.7 reduce_sum.18
  988.1 15.2 copy.30
  1003.3 8.6 bitcast_subtract_fusion
  1011.9 0.8 convolution_bitcast_fusion.3
  1012.7 48.8 %psum.15 = f32[128]{0:T(128)S(1)} all-reduce(f32[128]{0:T(128)S(1)} %convolution_bitcast_fusion.3), channel_id=1, replica_groups=mesh['ma'=8,'sa'=4] {'ma','sa'}, use_global_device_ids=true, to_apply=%region_7.8 | all-reduce | flops 128 | bytes 1024 | tf_op jit(solution)/shard_map/psum | solution.py:140
  1061.5 49.4 %all-reduce.6.cloned.1.call-done = f32[128,128]{1,0:T(8,128)} async-done(((f32[128,128]{1,0:T(8,128)}), f32[128,128]{1,0:T(8,128)}) %all-reduce.6.cloned.1.call-update) | async-done | bytes 65552 | tf_op jit(solution)/shard_map/psum | solution.py:140
  1110.9 0.9 multiply_add_fusion
  1111.8 201.6 %while.33 = (s32[]{:T(128)}, f32[128,128]{1,0:T(8,128)S(1)}, f32[128,128]{0,1:T(8,128)S(1)}, s32[]{:T(128)}, s32[]{:T(128)}) while((s32[]{:T(128)}, f32[128,128]{1,0:T(8,128)S(1)}, f32[128,128]{0,1:T(8,128)S(1)}, s32[]{:T(128)}, s32[]{:T(128)}) %tuple.85), condition=%wide.region_4.5_spmd.clone.clone, body=%wide.region_3.4_spmd.clone.clone.sunk | while | flops 246915 | bytes 332648 | solution.py:81
  1313.4 185.0 %while.32 = (s32[]{:T(128)}, f32[128,128]{1,0:T(8,128)S(1)}, f32[128,128]{1,0:T(8,128)S(1)}, s32[]{:T(128)}, s32[]{:T(128)}, /*index=5*/s32[]{:T(128)}) while((s32[]{:T(128)}, f32[128,128]{1,0:T(8,128)S(1)}, f32[128,128]{1,0:T(8,128)S(1)}, s32[]{:T(128)}, s32[]{:T(128)}, /*index=5*/s32[]{:T(128)}) %tuple.88), condition=%wide.region_6.7_spmd.clone, body=%wide.region_5.6_spmd.clone.sunk | while | flops 246404 | bytes 200048 | solution.py:95
  1498.8 21.7 %convolution_add_fusion = f32[128,32,1024]{2,0,1:T(8,128)} fusion(f32[128,32,1024]{2,0,1:T(8,128)} %bitcast_subtract_fusion, f32[32,1024]{1,0:T(8,128)S(1)} %broadcast_multiply_fusion, f32[128,128]{1,0:T(8,128)S(1)} %get-tuple-element.215, f32[128]{0:T(128)S(1)} %fusion.98), kind=kOutput, calls=%fused_computation.119 | convolution fusion | flops 6446661632 | bytes 33751552 | tf_op jit(solution)/shard_map/jxc,jk->kxc/dot_general | solution.py:63
  1520.5 15.5 copy.31
  1536.0 368.8 %all_to_all.23 = f32[128,32,1024]{2,1,0:T(8,128)S(1)} all-to-all(f32[128,32,1024]{2,1,0:T(8,128)S(1)} %copy.31), channel_id=1, replica_groups=mesh['ma'=8,'sa'=4] {'ma'}, dimensions={0} | all-to-all | bytes 33554432 | tf_op jit(solution)/shard_map/all_to_all | solution.py:151
  1904.8 6.2 copy.35
  (1317 shorter events, 299.4 us)
Async XLA Ops:
  33.6 23.3 %copy-start.1 = (f32[32,8192]{1,0:T(8,128)S(1)}, f32[32,8192]{1,0:T(8,128)}, u32[]{:S(2)}) copy-start(f32[32,8192]{1,0:T(8,128)} %param.12) | copy-start | bytes 3145732
  33.6 39.4 %copy-start.6 = (s32[16,2]{0,1:T(2,128)S(1)}, s32[16,2]{0,1:T(2,128)}, u32[]{:S(2)}) copy-start(s32[16,2]{0,1:T(2,128)} %param.13) | copy-start | bytes 388
  33.6 39.5 %copy-start.7 = (s32[16,2]{0,1:T(2,128)S(1)}, s32[16,2]{0,1:T(2,128)}, u32[]{:S(2)}) copy-start(s32[16,2]{0,1:T(2,128)} %param.14) | copy-start | bytes 388
  66.0 8.2 collective-permute-start
  71.1 6.1 collective-permute-start.1
  106.2 3.5 copy-start
  149.6 179.5 %copy-start.2 = (f32[16,32,128]{2,1,0:T(8,128)S(1)}, f32[16,32,128]{2,1,0:T(8,128)}, u32[]{:S(2)}) copy-start(f32[16,32,128]{2,1,0:T(8,128)} %exponential_multiply_fusion.1) | copy-start | bytes 786436
  522.1 31.3 %copy-start.3 = (s32[32,64]{1,0:T(8,128)S(1)}, s32[32,64]{1,0:T(8,128)}, u32[]{:S(2)}) copy-start(s32[32,64]{1,0:T(8,128)} %param.15) | copy-start | bytes 24580
  547.4 359.2 %all-to-all-start = ((f32[8,16,32,1024]{3,2,1,0:T(8,128)}), f32[8,16,32,1024]{3,2,1,0:T(8,128)}, u32[]{:S(2)}, u32[]{:S(2)}) async-start(f32[8,16,32,1024]{3,2,1,0:T(8,128)} %fusion.85), calls=%async_computation | async-start | bytes 33554432 | tf_op jit(solution)/shard_map/all_to_all | solution.py:116
  553.3 557.6 %all-reduce.6.cloned.1.call-start = ((), (), s32[]{:S(2)}) async-start(), calls=%async_computation.2 | async-start | bytes 131072 | tf_op jit(solution)/shard_map/psum | solution.py:140
  957.7 20.3 %copy-start.4 = (f32[32,64]{1,0:T(8,128)S(1)}, f32[32,64]{1,0:T(8,128)}, u32[]{:S(2)}) copy-start(f32[32,64]{1,0:T(8,128)} %param.16) | copy-start | bytes 24580
  957.7 20.3 %copy-start.5 = (f32[32,64]{1,0:T(8,128)S(1)}, f32[32,64]{1,0:T(8,128)}, u32[]{:S(2)}) copy-start(f32[32,64]{1,0:T(8,128)} %param.17) | copy-start | bytes 24580
Sparse Core Ops, SparseCore 0:
  981.5 129.2 all-reduce.5
